TPU v7x, 32 devices: a whole 2x2x4 slice. The times are simulated.
32 devices in a mesh: expert: 16 (over z, y, core), dp: 2 (over x).
Axes of the slice: x: 2, y: 2, z: 4, core: 2. Of those that a mesh axis runs over, the one named last changes fastest.
Arguments:
- tokens: bfloat16 [2, 512, 2048], P('dp', 'expert'), may hold values from -6 to 6
- cotangent: bfloat16 [2, 512, 2048], P('dp', 'expert'), may hold values from -6 to 6
- expert_ids: int32 [2, 512, 8], P('dp', 'expert'), may hold values from 0 to 15, all different within a row; in each aligned block of 32 rows (0 to 31, 32 to 63, ..., all dimensions but the last counted through in order) at most 24 rows name the same one
- gate_probs: bfloat16 [2, 512, 8], P('dp', 'expert'), may hold values from 0.029907227 to 0.59765625
- alpha: float32 [1], replicated, may hold values from 0.4 to 1.2
- gamma: float32 [2048], replicated, may hold values from 0.5 to 1.5
- beta: float32 [2048], replicated, may hold values from -1.5 to 1.5
- w_in: bfloat16 [16, 2, 768, 2048], P('expert', None, 'dp'), may hold values from -0.125 to 0.125
- w_down: bfloat16 [16, 768, 2048], P('expert', 'dp'), may hold values from -0.21875 to 0.21875
Outputs:
- grad_tokens: bfloat16 [2, 512, 2048], P('dp', 'expert')
- grad_probs: bfloat16 [2, 512, 8], P('dp', 'expert')
- grad_down: bfloat16 [16, 768, 2048], P('expert', 'dp')
- grad_gamma: float32 [2048], replicated
- grad_beta: float32 [2048], replicated
- grad_alpha: float32 [1], replicated
Inputs may be any that keep to these rules, and one draw needn't show every extreme that they name: `expert_ids`: each token names 8 different experts; among the 32 tokens of one block no expert is named by more than 24 tokens, and in some block some expert is named by exactly 24.
All inputs are finite; a program needn't handle non-finite values.
Results may differ from a plain program's by a relative error of at most 0.008.
Values may be sent and summed in bfloat16 or wider, within the bound.
No kernel may reach another device: no remote copies, remote signals or barrier semaphores. Data moves between devices by JAX's collectives and lax.ppermute only.
A program may use at most 64 MiB of HBM per device.

v0:
```python
import jax
import jax.numpy as jnp
from jax import lax
from jax.sharding import PartitionSpec as P

residual_scale = 0.7071


def contract_width(left, right):
    return lax.dot_general(
        left, right, (((1,), (1,)), ((), ())), preferred_element_type=jnp.float32
    )


def slot_layout(ids_local, expert_count, capacity):
    token_count, top_count = ids_local.shape
    labels = jnp.arange(expert_count, dtype=jnp.int32)
    onehot = (ids_local[:, :, None] == labels[None, None, :]).astype(jnp.int32)
    picks = jnp.sum(onehot, axis=1)
    before = jnp.cumsum(picks, axis=0) - picks
    slots = jnp.sum(onehot * before[:, None, :], axis=2)
    position = ids_local * capacity + slots
    pairs = jnp.arange(token_count * top_count, dtype=jnp.int32)
    table = jnp.full((expert_count * capacity,), token_count * top_count, jnp.int32)
    table = table.at[position.reshape(-1)].set(pairs)
    return (position, table)


def shards(tokens, cotangent, expert_ids, gate_probs, alpha, gamma, beta, w_in, w_down):
    expert_count = lax.axis_size("expert")
    token_count = tokens.shape[1]
    top_count = expert_ids.shape[2]
    width = tokens.shape[2]
    capacity = 3 * token_count * top_count // (2 * expert_count)
    rows_total = expert_count * capacity
    inputs = tokens[0].astype(jnp.float32)
    squashed = jnp.tanh(alpha[0] * inputs)
    normed = (gamma * squashed + beta).astype(jnp.bfloat16)
    position, table = slot_layout(expert_ids[0], expert_count, capacity)
    source_token = table // top_count
    zero_row = jnp.zeros((1, width), jnp.bfloat16)
    normed_pad = jnp.concatenate([normed, zero_row], axis=0)
    cot_pad = jnp.concatenate([cotangent[0], zero_row], axis=0)
    prob_pad = jnp.concatenate([gate_probs[0].reshape(-1), jnp.zeros((1,), jnp.bfloat16)], axis=0)
    send_rows = normed_pad[source_token].reshape(expert_count, capacity, width)
    send_cot = cot_pad[source_token].reshape(expert_count, capacity, width)
    send_prob = prob_pad[table].reshape(expert_count, capacity)
    recv_rows, recv_cot, recv_prob = (
        lax.all_to_all(send_rows, "expert", split_axis=0, concat_axis=0, tiled=True),
        lax.all_to_all(send_cot, "expert", split_axis=0, concat_axis=0, tiled=True),
        lax.all_to_all(send_prob, "expert", split_axis=0, concat_axis=0, tiled=True),
    )
    in_rows = recv_rows.reshape(rows_total, width)
    cot_rows = recv_cot.reshape(rows_total, width)
    prob_rows = recv_prob.reshape(rows_total).astype(jnp.float32)
    gate_up, lower_full = (
        lax.all_gather(w_in, "dp", axis=2, tiled=True),
        lax.all_gather(w_down, "dp", axis=1, tiled=True),
    )
    gate_pre = contract_width(in_rows, gate_up[0, 0])
    up_value = contract_width(in_rows, gate_up[0, 1])
    w_gate = gate_up[0, 0]
    w_upper = gate_up[0, 1]
    w_lower = lower_full[0]
    sigma = jax.nn.sigmoid(gate_pre)
    activation = (gate_pre * sigma * up_value).astype(jnp.bfloat16)
    back = contract_width(cot_rows, w_lower)
    weight_row = residual_scale * prob_rows
    scaled_cot = (weight_row[:, None] * cot_rows.astype(jnp.float32)).astype(jnp.bfloat16)
    row_grad = residual_scale * jnp.sum(activation.astype(jnp.float32) * back, axis=1)
    d_act = weight_row[:, None] * back
    d_gate = (d_act * up_value * sigma * (1.0 + gate_pre * (1.0 - sigma))).astype(jnp.bfloat16)
    d_up = (d_act * gate_pre * sigma).astype(jnp.bfloat16)
    d_rows = (
        jnp.dot(d_gate, w_gate, preferred_element_type=jnp.float32)
        + jnp.dot(d_up, w_upper, preferred_element_type=jnp.float32)
    ).astype(jnp.bfloat16)
    back_rows, back_probs = (
        lax.all_to_all(
            d_rows.reshape(expert_count, capacity, width),
            "expert",
            split_axis=0,
            concat_axis=0,
            tiled=True,
        ),
        lax.all_to_all(
            row_grad.astype(jnp.bfloat16).reshape(expert_count, capacity),
            "expert",
            split_axis=0,
            concat_axis=0,
            tiled=True,
        ),
    )
    partial_grad = lax.dot_general(
        activation, scaled_cot, (((0,), (0,)), ((), ())), preferred_element_type=jnp.float32
    )
    grad_down = lax.psum_scatter(
        partial_grad[None].astype(jnp.bfloat16), "dp", scatter_dimension=1, tiled=True
    )
    picked = back_rows.reshape(rows_total, width)[position]
    grad_normed = jnp.sum(picked.astype(jnp.float32), axis=1)
    grad_probs = back_probs.reshape(rows_total)[position]
    gamma_part = jnp.sum(grad_normed * squashed, axis=0)
    beta_part = jnp.sum(grad_normed, axis=0)
    pre_grad = grad_normed * gamma * (1.0 - squashed * squashed)
    alpha_part = jnp.sum(pre_grad * inputs).reshape(1)
    grad_gamma, grad_beta, grad_alpha = lax.psum(
        (gamma_part, beta_part, alpha_part), ("expert", "dp")
    )
    grad_tokens = (cotangent[0].astype(jnp.float32) + alpha[0] * pre_grad).astype(jnp.bfloat16)
    return (grad_tokens[None], grad_probs[None], grad_down, grad_gamma, grad_beta, grad_alpha)


def solution(mesh):
    placed = (
        P("dp", "expert", None),
        P("dp", "expert", None),
        P("dp", "expert", None),
        P("dp", "expert", None),
        P(),
        P(),
        P(),
        P("expert", None, "dp", None),
        P("expert", "dp", None),
    )
    return jax.shard_map(
        shards,
        mesh=mesh,
        in_specs=placed,
        out_specs=(
            P("dp", "expert", None),
            P("dp", "expert", None),
            P("expert", "dp", None),
            P(),
            P(),
            P(),
        ),
        check_vma=False,
    )
```

profile of v0, /device:TPU:0, one launch (start us, length us, event | category | flops | bytes accessed | tf_op | source)
XLA Modules:
  0.0 256.3 jit_solution(2240395038127851113)
XLA Ops:
  7.3 0.7 all-gather.5.cloned.1.call-update
  8.0 0.1 copy.30
  8.1 0.1 reshape_squeeze.3
  8.2 0.1 copy.32
  8.3 0.1 copy.31
  8.3 0.1 mul.162
  8.5 0.1 copy.34
  8.6 0.1 copy.35
  8.7 0.1 reduce_sum.71
  8.8 1.4 scatter_custom_fusion
  10.2 2.8 %gather_fusion = bf16[384]{0:T(512)(128)(2,1)S(1)} fusion(bf16[257]{0:T(512)(128)(2,1)S(1)} %pad_maximum_fusion, s32[1024]{0:T(1024)S(1)} %get-tuple-element.35), kind=kCustom, calls=%fused_computation | custom fusion | bytes 3072 | tf_op jit(solution)/shard_map/gather | solution.py:47
  13.1 0.7 all_to_all.25
  13.8 7.4 %all-to-all-start = ((bf16[16,1,24]{2,1,0:T(2,128)(2,1)}), bf16[16,1,24]{2,1,0:T(2,128)(2,1)S(1)}, u32[]{:S(2)}, u32[]{:S(2)}) async-start(bf16[16,1,24]{2,1,0:T(2,128)(2,1)} %all_to_all.25), calls=%async_computation | async-start | bytes 16384 | tf_op jit(solution)/shard_map/all_to_all | solution.py:51
  21.8 0.1 fusion.19
  21.9 3.1 %gather_fusion.2 = bf16[384,2048]{1,0:T(8,128)(2,1)} fusion(bf16[33,2048]{1,0:T(8,128)(2,1)S(1)} %concatenate.11, s32[1024]{0:T(1024)S(1)} %get-tuple-element.34), kind=kCustom, calls=%fused_computation.2 | custom fusion | bytes 3147264 | tf_op jit(solution)/shard_map/gather | solution.py:45
  25.0 2.4 all-to-all-done
  27.5 3.7 %all-to-all-start.2 = ((bf16[16,24,2048]{2,1,0:T(8,128)(2,1)}), bf16[16,24,2048]{2,1,0:T(8,128)(2,1)S(1)}, u32[]{:S(2)}, u32[]{:S(2)}) async-start(bf16[16,24,2048]{2,1,0:T(8,128)(2,1)} %bitcast.8), calls=%async_computation.2 | async-start | bytes 3145728 | tf_op jit(solution)/shard_map/all_to_all | solution.py:49
  31.3 0.7 all-gather.3.cloned.1.call-update
  32.0 0.1 copy-done.1
  32.1 3.1 %gather_fusion.1 = bf16[384,2048]{1,0:T(8,128)(2,1)} fusion(bf16[33,2048]{1,0:T(8,128)(2,1)S(1)} %concatenate.10, s32[1024]{0:T(1024)S(1)} %get-tuple-element.34), kind=kCustom, calls=%fused_computation.1 | custom fusion | bytes 3147264 | tf_op jit(solution)/shard_map/gather | solution.py:46
  35.3 27.8 %all-to-all-done.2 = bf16[16,24,2048]{2,1,0:T(8,128)(2,1)S(1)} async-done(((bf16[16,24,2048]{2,1,0:T(8,128)(2,1)}), bf16[16,24,2048]{2,1,0:T(8,128)(2,1)S(1)}, u32[]{:S(2)}, u32[]{:S(2)}) %all-to-all-start.2) | async-done | bytes 1572896 | tf_op jit(solution)/shard_map/all_to_all | solution.py:49
  63.1 9.1 %all-to-all-start.1 = ((bf16[16,24,2048]{2,1,0:T(8,128)(2,1)}), bf16[16,24,2048]{2,1,0:T(8,128)(2,1)S(1)}, u32[]{:S(2)}, u32[]{:S(2)}) async-start(bf16[16,24,2048]{2,1,0:T(8,128)(2,1)} %bitcast.4), calls=%async_computation.1 | async-start | bytes 3145728 | tf_op jit(solution)/shard_map/all_to_all | solution.py:50
  72.3 0.1 mul.166
  72.4 20.3 %all-gather.5.cloned.1.call-done = bf16[1,2,768,2048]{3,2,1,0:T(8,128)(2,1)} async-done(((bf16[1,2,384,2048]{3,2,1,0:T(8,128)(2,1)}), bf16[1,2,768,2048]{3,2,1,0:T(8,128)(2,1)}) %all-gather.5.cloned.1.call-update) | async-done | bytes 6291472 | tf_op jit(solution)/shard_map/all_gather | solution.py:57
  92.7 4.6 %fusion.5 = f32[384,768]{1,0:T(8,128)} fusion(bf16[384,2048]{1,0:T(8,128)(2,1)S(1)} %bitcast.79, bf16[1,2,768,2048]{3,2,1,0:T(8,128)(2,1)} %all-gather.5.cloned.1.call-done), kind=kOutput, calls=%fused_computation.16 | convolution fusion | flops 1207959552 | bytes 5898240 | tf_op jit(solution)/shard_map/dot_general | solution.py:10
  97.3 2.5 fusion.3
  99.8 4.4 %all-to-all-done.1 = bf16[16,24,2048]{2,1,0:T(8,128)(2,1)S(1)} async-done(((bf16[16,24,2048]{2,1,0:T(8,128)(2,1)}), bf16[16,24,2048]{2,1,0:T(8,128)(2,1)S(1)}, u32[]{:S(2)}, u32[]{:S(2)}) %all-to-all-start.1) | async-done | bytes 1572896 | tf_op jit(solution)/shard_map/all_to_all | solution.py:50
  104.2 35.0 %all-gather.3.cloned.1.call-done = bf16[1,768,2048]{2,1,0:T(8,128)(2,1)} async-done(((bf16[1,384,2048]{2,1,0:T(8,128)(2,1)}), bf16[1,768,2048]{2,1,0:T(8,128)(2,1)}) %all-gather.3.cloned.1.call-update) | async-done | bytes 3145744 | tf_op jit(solution)/shard_map/all_gather | solution.py:58
  139.2 5.0 %multiply_reduce_fusion = (f32[384]{0:T(512)S(1)}, bf16[384,768]{1,0:T(8,128)(2,1)S(1)}, f32[384,768]{1,0:T(8,128)}) fusion(f32[384,768]{1,0:T(8,128)} %fusion.3, f32[384,768]{1,0:T(8,128)} %fusion.5, bf16[384,2048]{1,0:T(8,128)(2,1)S(1)} %bitcast.81, bf16[1,768,2048]{2,1,0:T(8,128)(2,1)} %all-gather.3.cloned.1.call-done), kind=kOutput, calls=%fused_computation.21 | convolution fusion | flops 1210613376 | bytes 8848896 | tf_op jit(solution)/shard_map/dot_general | solution.py:10
  144.2 3.6 %fusion.2 = bf16[1,768,2048]{2,1,0:T(8,128)(2,1)} fusion(bf16[384,768]{1,0:T(8,128)(2,1)S(1)} %get-tuple-element.30, bf16[384,2048]{1,0:T(8,128)(2,1)S(1)} %bitcast.82, f32[384]{0:T(512)S(1)} %mul.166), kind=kOutput, calls=%fused_computation.13 | convolution fusion | flops 1211891712 | bytes 5309952 | tf_op jit(solution)/shard_map/dot_general | solution.py:94
  147.9 0.7 convert_element_type.97
  148.6 5.6 %all-to-all-start.4 = ((bf16[16,1,24]{2,1,0:T(2,128)(2,1)}), bf16[16,1,24]{2,1,0:T(2,128)(2,1)S(1)}, u32[]{:S(2)}, u32[]{:S(2)}) async-start(bf16[16,1,24]{2,1,0:T(2,128)(2,1)} %convert_element_type.97), calls=%async_computation.4 | async-start | bytes 16384 | tf_op jit(solution)/shard_map/all_to_all | solution.py:86
  154.3 4.4 %fusion.4 = f32[384,2048]{1,0:T(8,128)S(1)} fusion(bf16[1,2,768,2048]{3,2,1,0:T(8,128)(2,1)} %all-gather.5.cloned.1.call-done, f32[384,768]{1,0:T(8,128)S(1)} %copy-done.8, f32[384,768]{1,0:T(8,128)S(1)} %copy-done.9, f32[384,768]{1,0:T(8,128)} %get-tuple-element.33, f32[384]{0:T(512)S(1)} %mul.166), kind=kOutput, calls=%fused_computation.15 | convolution fusion | flops 1211203584 | bytes 9831936 | tf_op jit(solution)/shard_map/dot_general | solution.py:75
  158.7 4.7 %add_convert_fusion = bf16[384,2048]{1,0:T(8,128)(2,1)} fusion(f32[384,2048]{1,0:T(8,128)S(1)} %fusion.4, bf16[1,2,768,2048]{3,2,1,0:T(8,128)(2,1)} %all-gather.5.cloned.1.call-done, f32[384,768]{1,0:T(8,128)S(1)} %copy-done.8, f32[384,768]{1,0:T(8,128)S(1)} %copy-done.10, f32[384]{0:T(512)S(1)} %mul.166), kind=kOutput, calls=%fused_computation.12 | convolution fusion | flops 1211596800 | bytes 10225152 | tf_op jit(solution)/shard_map/dot_general | solution.py:76
  163.4 6.0 %all-to-all-start.3 = ((bf16[16,24,2048]{2,1,0:T(8,128)(2,1)}), bf16[16,24,2048]{2,1,0:T(8,128)(2,1)S(1)}, u32[]{:S(2)}, u32[]{:S(2)}) async-start(bf16[16,24,2048]{2,1,0:T(8,128)(2,1)} %bitcast.12), calls=%async_computation.3 | async-start | bytes 3145728 | tf_op jit(solution)/shard_map/all_to_all | solution.py:79
  169.4 0.1 copy.37
  169.5 0.1 reshape.211
  169.6 0.1 reshape.182
  169.7 1.9 gather_fusion.4
  171.7 0.1 broadcast_in_dim.11
  171.8 0.7 copy.39
  172.4 28.9 %all-to-all-done.3 = bf16[16,24,2048]{2,1,0:T(8,128)(2,1)S(1)} async-done(((bf16[16,24,2048]{2,1,0:T(8,128)(2,1)}), bf16[16,24,2048]{2,1,0:T(8,128)(2,1)S(1)}, u32[]{:S(2)}, u32[]{:S(2)}) %all-to-all-start.3) | async-done | bytes 1572896 | tf_op jit(solution)/shard_map/all_to_all | solution.py:79
  201.4 1.4 gather_fusion.3
  202.8 0.7 fusion.6
  203.4 0.7 fusion.23
  204.2 0.2 convert_reduce_fusion
  204.3 44.7 %all-reduce.2 = (f32[2048]{0:T(1024)}, f32[2048]{0:T(1024)}, f32[1]{0:T(128)}) all-reduce(f32[2048]{0:T(1024)S(1)} %get-tuple-element.25, f32[2048]{0:T(1024)S(1)} %convert_reduce_fusion, f32[1]{0:T(128)} %bitcast.19), channel_id=1, replica_groups=mesh['expert'=16,'dp'=2] {'expert','dp'}, use_global_device_ids=true, to_apply=%region_8.9 | all-reduce | flops 4097 | bytes 32776 | tf_op jit(solution)/shard_map/psum | solution.py:107
  249.0 0.8 fusion.30
  (44 shorter events, 0.4 us)
Async XLA Ops:
  7.2 0.8 copy-start.6
  7.2 1.0 copy-start.4
  7.2 14.6 %copy-start = (bf16[1,32,2048]{2,1,0:T(8,128)(2,1)S(1)}, bf16[1,32,2048]{2,1,0:T(8,128)(2,1)}, u32[]{:S(2)}) copy-start(bf16[1,32,2048]{2,1,0:T(8,128)(2,1)} %param.9) | copy-start | bytes 393220
  7.2 14.6 %copy-start.3 = (f32[2048]{0:T(1024)S(1)}, f32[2048]{0:T(1024)}, u32[]{:S(2)}) copy-start(f32[2048]{0:T(1024)} %param.14) | copy-start | bytes 24580
  7.2 14.6 %copy-start.5 = (f32[2048]{0:T(1024)S(1)}, f32[2048]{0:T(1024)}, u32[]{:S(2)}) copy-start(f32[2048]{0:T(1024)} %param.15) | copy-start | bytes 24580
  7.2 85.5 %all-gather.5.cloned.1.call-start = ((), (), s32[]{:S(2)}) async-start(), calls=%async_computation.7 | async-start | bytes 9437184 | tf_op jit(solution)/shard_map/all_gather | solution.py:57
  13.8 13.7 %all-to-all-start = ((bf16[16,1,24]{2,1,0:T(2,128)(2,1)}), bf16[16,1,24]{2,1,0:T(2,128)(2,1)S(1)}, u32[]{:S(2)}, u32[]{:S(2)}) async-start(bf16[16,1,24]{2,1,0:T(2,128)(2,1)} %all_to_all.25), calls=%async_computation | async-start | bytes 16384 | tf_op jit(solution)/shard_map/all_to_all | solution.py:51
  27.5 35.6 %all-to-all-start.2 = ((bf16[16,24,2048]{2,1,0:T(8,128)(2,1)}), bf16[16,24,2048]{2,1,0:T(8,128)(2,1)S(1)}, u32[]{:S(2)}, u32[]{:S(2)}) async-start(bf16[16,24,2048]{2,1,0:T(8,128)(2,1)} %bitcast.8), calls=%async_computation.2 | async-start | bytes 3145728 | tf_op jit(solution)/shard_map/all_to_all | solution.py:49
  31.2 0.9 copy-start.1
  31.2 108.0 %all-gather.3.cloned.1.call-start = ((), (), s32[]{:S(2)}) async-start(), calls=%async_computation.6 | async-start | bytes 4718592 | tf_op jit(solution)/shard_map/all_gather | solution.py:58
  63.1 41.1 %all-to-all-start.1 = ((bf16[16,24,2048]{2,1,0:T(8,128)(2,1)}), bf16[16,24,2048]{2,1,0:T(8,128)(2,1)S(1)}, u32[]{:S(2)}, u32[]{:S(2)}) async-start(bf16[16,24,2048]{2,1,0:T(8,128)(2,1)} %bitcast.4), calls=%async_computation.1 | async-start | bytes 3145728 | tf_op jit(solution)/shard_map/all_to_all | solution.py:50
  72.2 177.6 %reduce-scatter.2.cloned.1.call-start = ((), (), s32[]{:S(2)}) async-start(), calls=%async_computation.8 | async-start | bytes 4718592 | tf_op jit(solution)/shard_map/reduce_scatter | solution.py:97
  92.7 4.6 %copy-start.7 = (bf16[1,2,768,2048]{3,2,1,0:T(8,128)(2,1)S(1)}, bf16[1,2,768,2048]{3,2,1,0:T(8,128)(2,1)}, u32[]{:S(2)}) copy-start(bf16[1,2,768,2048]{3,2,1,0:T(8,128)(2,1)} %all-gather.5.cloned.1.call-done) | copy-start | bytes 18874372
  147.9 6.4 %copy-start.8 = (f32[384,768]{1,0:T(8,128)S(1)}, f32[384,768]{1,0:T(8,128)}, u32[]{:S(2)}) copy-start(f32[384,768]{1,0:T(8,128)} %fusion.5) | copy-start | bytes 3538948
  147.9 6.4 %copy-start.9 = (f32[384,768]{1,0:T(8,128)S(1)}, f32[384,768]{1,0:T(8,128)}, u32[]{:S(2)}) copy-start(f32[384,768]{1,0:T(8,128)} %fusion.3) | copy-start | bytes 3538948
  148.6 14.8 %all-to-all-start.4 = ((bf16[16,1,24]{2,1,0:T(2,128)(2,1)}), bf16[16,1,24]{2,1,0:T(2,128)(2,1)S(1)}, u32[]{:S(2)}, u32[]{:S(2)}) async-start(bf16[16,1,24]{2,1,0:T(2,128)(2,1)} %convert_element_type.97), calls=%async_computation.4 | async-start | bytes 16384 | tf_op jit(solution)/shard_map/all_to_all | solution.py:86
  154.2 4.4 %copy-start.10 = (f32[384,768]{1,0:T(8,128)S(1)}, f32[384,768]{1,0:T(8,128)}, u32[]{:S(2)}) copy-start(f32[384,768]{1,0:T(8,128)} %get-tuple-element.33) | copy-start | bytes 3538948
  163.4 38.0 %all-to-all-start.3 = ((bf16[16,24,2048]{2,1,0:T(8,128)(2,1)}), bf16[16,24,2048]{2,1,0:T(8,128)(2,1)S(1)}, u32[]{:S(2)}, u32[]{:S(2)}) async-start(bf16[16,24,2048]{2,1,0:T(8,128)(2,1)} %bitcast.12), calls=%async_computation.3 | async-start | bytes 3145728 | tf_op jit(solution)/shard_map/all_to_all | solution.py:79
  202.7 46.3 %copy-start.2 = (bf16[1,32,2048]{2,1,0:T(8,128)(2,1)S(1)}, bf16[1,32,2048]{2,1,0:T(8,128)(2,1)}, u32[]{:S(2)}) copy-start(bf16[1,32,2048]{2,1,0:T(8,128)(2,1)} %param.10) | copy-start | bytes 393220
Sparse Core Ops, SparseCore 0:
  9.6 83.0 all-gather.4
  94.2 44.9 all-gather.2
  148.0 43.3 reduce-scatter.1
where the time goes:
time: 257 us; the launch traced here: 256 us
  waiting for transfers between devices  120 us (47%)
  blocking collectives  44.7 us (17%)
  starting transfers between devices  31.9 us (12%)
  matrix products  24.8 us (10%)
  local copies, waits for them, and re-layouts  17.1 us (7%)
  between operations  14.7 us (6%)
  other arithmetic  2.6 us (1%)
    psum x1, blocking collectives, shards(): lax.psum((gamma_part, beta_part, alpha_part), ('expert', 'dp'))  44.7 us
    all_gather x1, waiting for transfers between devices, shards(): lax.all_gather(w_down, 'dp', axis=1, tiled=True)  35 us
    all_to_all x1, waiting for transfers between devices, shards(): lax.all_to_all(d_rows.reshape(expert_count, capacity, width), 'expert', s...  28.9 us
    all_to_all x1, waiting for transfers between devices, shards(): lax.all_to_all(send_rows, 'expert', split_axis=0, concat_axis=0, tiled=True)  27.8 us
    all_gather x1, waiting for transfers between devices, shards(): lax.all_gather(w_in, 'dp', axis=2, tiled=True)  20.3 us
    dot_general x3, matrix products, contract_width(): lax.dot_general(left, right, (((1,), (1,)), ((), ())), preferred_element_...  12.1 us
    all_to_all x1, starting transfers between devices, shards(): lax.all_to_all(send_cot, 'expert', split_axis=0, concat_axis=0, tiled=True)  9.08 us
    all_to_all x1, starting transfers between devices, shards(): lax.all_to_all(send_prob, 'expert', split_axis=0, concat_axis=0, tiled=True)  7.39 us
  transfers between devices with their start and end apart: 8, of which 6 were waited for; matrix products, arithmetic and copies ran while one was open for 14% of the time, Pallas kernels for 0%

commit v1 on v0

--- a/solution.py
+++ b/solution.py
@@ -4,6 +4,12 @@
 from jax.sharding import PartitionSpec as P
 
 residual_scale = 0.7071
+
+
+def group_panels(row_data, device_axis, named_axis):
+    for t in (device_axis, named_axis):
+        row_data = lax.psum(row_data, t)
+    return row_data
 
 
 def contract_width(left, right):
@@ -104,8 +110,8 @@
     beta_part = jnp.sum(grad_normed, axis=0)
     pre_grad = grad_normed * gamma * (1.0 - squashed * squashed)
     alpha_part = jnp.sum(pre_grad * inputs).reshape(1)
-    grad_gamma, grad_beta, grad_alpha = lax.psum(
-        (gamma_part, beta_part, alpha_part), ("expert", "dp")
+    grad_gamma, grad_beta, grad_alpha = group_panels(
+        (gamma_part, beta_part, alpha_part), "dp", "expert"
     )
     grad_tokens = (cotangent[0].astype(jnp.float32) + alpha[0] * pre_grad).astype(jnp.bfloat16)
     return (grad_tokens[None], grad_probs[None], grad_down, grad_gamma, grad_beta, grad_alpha)

time: 257 us -> 284 us (1.11)
  blocking collectives: 44.7 us -> 72 us
    psum x1 -> x2, blocking collectives: 44.7 us -> 72 us  [group_panels(): row_data = lax.psum(row_data, t)]
  transfers between devices with their start and end apart: 8 -> 8, of which waited for: 6 -> 6; matrix products, arithmetic and copies ran while one was open for 14% -> 12% of each run, Pallas kernels for 0% -> 0%
where the time goes in v1:
time: 284 us
  waiting for transfers between devices  120 us (42%)
  blocking collectives  72 us (25%)
  starting transfers between devices  31.9 us (11%)
  matrix products  24.8 us (9%)
  local copies, waits for them, and re-layouts  17.1 us (6%)
  between operations  14.7 us (5%)
    psum x2, blocking collectives, group_panels(): row_data = lax.psum(row_data, t)  72 us
    all_gather x1, waiting for transfers between devices, shards(): lax.all_gather(w_down, 'dp', axis=1, tiled=True)  35 us
    all_to_all x1, waiting for transfers between devices, shards(): lax.all_to_all(d_rows.reshape(expert_count, capacity, width), 'expert', s...  28.9 us
    all_to_all x1, waiting for transfers between devices, shards(): lax.all_to_all(send_rows, 'expert', split_axis=0, concat_axis=0, tiled=True)  27.8 us
    all_gather x1, waiting for transfers between devices, shards(): lax.all_gather(w_in, 'dp', axis=2, tiled=True)  20.3 us
    dot_general x3, matrix products, contract_width(): lax.dot_general(left, right, (((1,), (1,)), ((), ())), preferred_element_...  12.1 us
    all_to_all x1, starting transfers between devices, shards(): lax.all_to_all(send_cot, 'expert', split_axis=0, concat_axis=0, tiled=True)  9.08 us
    all_to_all x1, starting transfers between devices, shards(): lax.all_to_all(send_prob, 'expert', split_axis=0, concat_axis=0, tiled=True)  7.39 us
  transfers between devices with their start and end apart: 8, of which 6 were waited for; matrix products, arithmetic and copies ran while one was open for 12% of the time, Pallas kernels for 0%

profile of v1, /device:TPU:0, one launch (start us, length us, event | category | flops | bytes accessed | tf_op | source)
XLA Modules:
  0.0 283.7 jit_solution(17510254273383719763)
XLA Ops:
  7.3 0.7 all-gather.5.cloned.1.call-update
  8.0 0.1 copy.30
  8.1 0.1 reshape_squeeze.3
  8.2 0.1 copy.32
  8.3 0.1 copy.31
  8.3 0.1 mul.162
  8.5 0.1 copy.34
  8.6 0.1 copy.35
  8.7 0.1 reduce_sum.71
  8.8 1.4 scatter_custom_fusion
  10.2 2.8 gather_fusion
  13.1 0.7 all_to_all.25
  13.8 7.4 %all-to-all-start = ((bf16[16,1,24]{2,1,0:T(2,128)(2,1)}), bf16[16,1,24]{2,1,0:T(2,128)(2,1)S(1)}, u32[]{:S(2)}, u32[]{:S(2)}) async-start(bf16[16,1,24]{2,1,0:T(2,128)(2,1)} %all_to_all.25), calls=%async_computation | async-start | bytes 16384 | tf_op jit(solution)/shard_map/all_to_all | solution.py:57
  21.9 3.1 %gather_fusion.2 = bf16[384,2048]{1,0:T(8,128)(2,1)} fusion(bf16[33,2048]{1,0:T(8,128)(2,1)S(1)} %concatenate.11, s32[1024]{0:T(1024)S(1)} %get-tuple-element.37), kind=kCustom, calls=%fused_computation.2 | custom fusion | bytes 3147264 | tf_op jit(solution)/shard_map/gather | solution.py:51
  25.0 2.4 all-to-all-done
  27.5 3.7 %all-to-all-start.2 = ((bf16[16,24,2048]{2,1,0:T(8,128)(2,1)}), bf16[16,24,2048]{2,1,0:T(8,128)(2,1)S(1)}, u32[]{:S(2)}, u32[]{:S(2)}) async-start(bf16[16,24,2048]{2,1,0:T(8,128)(2,1)} %bitcast.8), calls=%async_computation.2 | async-start | bytes 3145728 | tf_op jit(solution)/shard_map/all_to_all | solution.py:55
  31.3 0.7 all-gather.3.cloned.1.call-update
  32.0 0.1 copy-done.1
  32.1 3.1 %gather_fusion.1 = bf16[384,2048]{1,0:T(8,128)(2,1)} fusion(bf16[33,2048]{1,0:T(8,128)(2,1)S(1)} %concatenate.10, s32[1024]{0:T(1024)S(1)} %get-tuple-element.37), kind=kCustom, calls=%fused_computation.1 | custom fusion | bytes 3147264 | tf_op jit(solution)/shard_map/gather | solution.py:52
  35.3 27.8 %all-to-all-done.2 = bf16[16,24,2048]{2,1,0:T(8,128)(2,1)S(1)} async-done(((bf16[16,24,2048]{2,1,0:T(8,128)(2,1)}), bf16[16,24,2048]{2,1,0:T(8,128)(2,1)S(1)}, u32[]{:S(2)}, u32[]{:S(2)}) %all-to-all-start.2) | async-done | bytes 1572896 | tf_op jit(solution)/shard_map/all_to_all | solution.py:55
  63.1 9.1 %all-to-all-start.1 = ((bf16[16,24,2048]{2,1,0:T(8,128)(2,1)}), bf16[16,24,2048]{2,1,0:T(8,128)(2,1)S(1)}, u32[]{:S(2)}, u32[]{:S(2)}) async-start(bf16[16,24,2048]{2,1,0:T(8,128)(2,1)} %bitcast.4), calls=%async_computation.1 | async-start | bytes 3145728 | tf_op jit(solution)/shard_map/all_to_all | solution.py:56
  72.3 0.1 mul.166
  72.4 20.3 %all-gather.5.cloned.1.call-done = bf16[1,2,768,2048]{3,2,1,0:T(8,128)(2,1)} async-done(((bf16[1,2,384,2048]{3,2,1,0:T(8,128)(2,1)}), bf16[1,2,768,2048]{3,2,1,0:T(8,128)(2,1)}) %all-gather.5.cloned.1.call-update) | async-done | bytes 6291472 | tf_op jit(solution)/shard_map/all_gather | solution.py:63
  92.7 4.5 %fusion.5 = f32[384,768]{1,0:T(8,128)} fusion(bf16[384,2048]{1,0:T(8,128)(2,1)S(1)} %bitcast.79, bf16[1,2,768,2048]{3,2,1,0:T(8,128)(2,1)} %all-gather.5.cloned.1.call-done), kind=kOutput, calls=%fused_computation.16 | convolution fusion | flops 1207959552 | bytes 5898240 | tf_op jit(solution)/shard_map/dot_general | solution.py:16
  97.2 2.6 fusion.3
  99.8 4.4 %all-to-all-done.1 = bf16[16,24,2048]{2,1,0:T(8,128)(2,1)S(1)} async-done(((bf16[16,24,2048]{2,1,0:T(8,128)(2,1)}), bf16[16,24,2048]{2,1,0:T(8,128)(2,1)S(1)}, u32[]{:S(2)}, u32[]{:S(2)}) %all-to-all-start.1) | async-done | bytes 1572896 | tf_op jit(solution)/shard_map/all_to_all | solution.py:56
  104.2 35.0 %all-gather.3.cloned.1.call-done = bf16[1,768,2048]{2,1,0:T(8,128)(2,1)} async-done(((bf16[1,384,2048]{2,1,0:T(8,128)(2,1)}), bf16[1,768,2048]{2,1,0:T(8,128)(2,1)}) %all-gather.3.cloned.1.call-update) | async-done | bytes 3145744 | tf_op jit(solution)/shard_map/all_gather | solution.py:64
  139.2 5.0 %multiply_reduce_fusion = (f32[384]{0:T(512)S(1)}, bf16[384,768]{1,0:T(8,128)(2,1)S(1)}, f32[384,768]{1,0:T(8,128)}) fusion(f32[384,768]{1,0:T(8,128)} %fusion.3, f32[384,768]{1,0:T(8,128)} %fusion.5, bf16[384,2048]{1,0:T(8,128)(2,1)S(1)} %bitcast.81, bf16[1,768,2048]{2,1,0:T(8,128)(2,1)} %all-gather.3.cloned.1.call-done), kind=kOutput, calls=%fused_computation.21 | convolution fusion | flops 1210613376 | bytes 8848896 | tf_op jit(solution)/shard_map/dot_general | solution.py:16
  144.2 3.6 %fusion.2 = bf16[1,768,2048]{2,1,0:T(8,128)(2,1)} fusion(bf16[384,768]{1,0:T(8,128)(2,1)S(1)} %get-tuple-element.33, bf16[384,2048]{1,0:T(8,128)(2,1)S(1)} %bitcast.82, f32[384]{0:T(512)S(1)} %mul.166), kind=kOutput, calls=%fused_computation.13 | convolution fusion | flops 1211891712 | bytes 5309952 | tf_op jit(solution)/shard_map/dot_general | solution.py:100
  147.9 0.7 convert_element_type.97
  148.6 5.6 %all-to-all-start.4 = ((bf16[16,1,24]{2,1,0:T(2,128)(2,1)}), bf16[16,1,24]{2,1,0:T(2,128)(2,1)S(1)}, u32[]{:S(2)}, u32[]{:S(2)}) async-start(bf16[16,1,24]{2,1,0:T(2,128)(2,1)} %convert_element_type.97), calls=%async_computation.4 | async-start | bytes 16384 | tf_op jit(solution)/shard_map/all_to_all | solution.py:92
  154.3 4.4 %fusion.4 = f32[384,2048]{1,0:T(8,128)S(1)} fusion(bf16[1,2,768,2048]{3,2,1,0:T(8,128)(2,1)} %all-gather.5.cloned.1.call-done, f32[384,768]{1,0:T(8,128)S(1)} %copy-done.8, f32[384,768]{1,0:T(8,128)S(1)} %copy-done.9, f32[384,768]{1,0:T(8,128)} %get-tuple-element.36, f32[384]{0:T(512)S(1)} %mul.166), kind=kOutput, calls=%fused_computation.15 | convolution fusion | flops 1211203584 | bytes 9831936 | tf_op jit(solution)/shard_map/dot_general | solution.py:81
  158.7 4.7 %add_convert_fusion = bf16[384,2048]{1,0:T(8,128)(2,1)} fusion(f32[384,2048]{1,0:T(8,128)S(1)} %fusion.4, bf16[1,2,768,2048]{3,2,1,0:T(8,128)(2,1)} %all-gather.5.cloned.1.call-done, f32[384,768]{1,0:T(8,128)S(1)} %copy-done.8, f32[384,768]{1,0:T(8,128)S(1)} %copy-done.10, f32[384]{0:T(512)S(1)} %mul.166), kind=kOutput, calls=%fused_computation.12 | convolution fusion | flops 1211596800 | bytes 10225152 | tf_op jit(solution)/shard_map/dot_general | solution.py:82
  163.4 6.0 %all-to-all-start.3 = ((bf16[16,24,2048]{2,1,0:T(8,128)(2,1)}), bf16[16,24,2048]{2,1,0:T(8,128)(2,1)S(1)}, u32[]{:S(2)}, u32[]{:S(2)}) async-start(bf16[16,24,2048]{2,1,0:T(8,128)(2,1)} %bitcast.12), calls=%async_computation.3 | async-start | bytes 3145728 | tf_op jit(solution)/shard_map/all_to_all | solution.py:85
  169.5 0.1 copy.37
  169.5 0.1 reshape.211
  169.7 0.1 reshape.182
  169.8 1.9 gather_fusion.4
  171.7 0.1 broadcast_in_dim.11
  171.8 0.7 copy.39
  172.5 28.9 %all-to-all-done.3 = bf16[16,24,2048]{2,1,0:T(8,128)(2,1)S(1)} async-done(((bf16[16,24,2048]{2,1,0:T(8,128)(2,1)}), bf16[16,24,2048]{2,1,0:T(8,128)(2,1)S(1)}, u32[]{:S(2)}, u32[]{:S(2)}) %all-to-all-start.3) | async-done | bytes 1572896 | tf_op jit(solution)/shard_map/all_to_all | solution.py:85
  201.4 1.4 gather_fusion.3
  202.8 0.7 fusion.6
  203.5 0.7 fusion.23
  204.2 0.2 convert_reduce_fusion
  204.4 8.9 %all-reduce.3 = (f32[2048]{0:T(1024)S(1)}, f32[2048]{0:T(1024)S(1)}, f32[1]{0:T(128)}) all-reduce(f32[2048]{0:T(1024)S(1)} %get-tuple-element.25, f32[2048]{0:T(1024)S(1)} %convert_reduce_fusion, f32[1]{0:T(128)} %bitcast.19), channel_id=1, replica_groups=mesh['expert'=16,'dp'=2] {'dp'}, use_global_device_ids=true, to_apply=%region_8.9 | all-reduce | flops 4097 | bytes 32776 | tf_op jit(solution)/shard_map/psum | solution.py:11
  213.3 63.1 %all-reduce.2 = (f32[2048]{0:T(1024)}, f32[2048]{0:T(1024)}, f32[1]{0:T(128)}) all-reduce(f32[2048]{0:T(1024)S(1)} %get-tuple-element.29, f32[2048]{0:T(1024)S(1)} %get-tuple-element.30, f32[1]{0:T(128)} %get-tuple-element.31), channel_id=1, replica_groups=mesh['expert'=16,'dp'=2] {'expert'}, use_global_device_ids=true, to_apply=%region_9.10 | all-reduce | flops 4097 | bytes 32776 | tf_op jit(solution)/shard_map/psum | solution.py:11
  276.4 0.8 fusion.30
  (45 shorter events, 0.5 us)
Async XLA Ops:
  7.2 0.8 copy-start.6
  7.2 1.0 copy-start.4
  7.2 14.6 %copy-start = (bf16[1,32,2048]{2,1,0:T(8,128)(2,1)S(1)}, bf16[1,32,2048]{2,1,0:T(8,128)(2,1)}, u32[]{:S(2)}) copy-start(bf16[1,32,2048]{2,1,0:T(8,128)(2,1)} %param.9) | copy-start | bytes 393220
  7.2 14.6 %copy-start.3 = (f32[2048]{0:T(1024)S(1)}, f32[2048]{0:T(1024)}, u32[]{:S(2)}) copy-start(f32[2048]{0:T(1024)} %param.14) | copy-start | bytes 24580
  7.2 14.6 %copy-start.5 = (f32[2048]{0:T(1024)S(1)}, f32[2048]{0:T(1024)}, u32[]{:S(2)}) copy-start(f32[2048]{0:T(1024)} %param.15) | copy-start | bytes 24580
  7.2 85.5 %all-gather.5.cloned.1.call-start = ((), (), s32[]{:S(2)}) async-start(), calls=%async_computation.7 | async-start | bytes 9437184 | tf_op jit(solution)/shard_map/all_gather | solution.py:63
  13.8 13.7 %all-to-all-start = ((bf16[16,1,24]{2,1,0:T(2,128)(2,1)}), bf16[16,1,24]{2,1,0:T(2,128)(2,1)S(1)}, u32[]{:S(2)}, u32[]{:S(2)}) async-start(bf16[16,1,24]{2,1,0:T(2,128)(2,1)} %all_to_all.25), calls=%async_computation | async-start | bytes 16384 | tf_op jit(solution)/shard_map/all_to_all | solution.py:57
  27.5 35.6 %all-to-all-start.2 = ((bf16[16,24,2048]{2,1,0:T(8,128)(2,1)}), bf16[16,24,2048]{2,1,0:T(8,128)(2,1)S(1)}, u32[]{:S(2)}, u32[]{:S(2)}) async-start(bf16[16,24,2048]{2,1,0:T(8,128)(2,1)} %bitcast.8), calls=%async_computation.2 | async-start | bytes 3145728 | tf_op jit(solution)/shard_map/all_to_all | solution.py:55
  31.2 0.9 copy-start.1
  31.2 108.0 %all-gather.3.cloned.1.call-start = ((), (), s32[]{:S(2)}) async-start(), calls=%async_computation.6 | async-start | bytes 4718592 | tf_op jit(solution)/shard_map/all_gather | solution.py:64
  63.1 41.1 %all-to-all-start.1 = ((bf16[16,24,2048]{2,1,0:T(8,128)(2,1)}), bf16[16,24,2048]{2,1,0:T(8,128)(2,1)S(1)}, u32[]{:S(2)}, u32[]{:S(2)}) async-start(bf16[16,24,2048]{2,1,0:T(8,128)(2,1)} %bitcast.4), calls=%async_computation.1 | async-start | bytes 3145728 | tf_op jit(solution)/shard_map/all_to_all | solution.py:56
  72.2 205.0 %reduce-scatter.2.cloned.1.call-start = ((), (), s32[]{:S(2)}) async-start(), calls=%async_computation.8 | async-start | bytes 4718592 | tf_op jit(solution)/shard_map/reduce_scatter | solution.py:103
  92.7 4.5 %copy-start.7 = (bf16[1,2,768,2048]{3,2,1,0:T(8,128)(2,1)S(1)}, bf16[1,2,768,2048]{3,2,1,0:T(8,128)(2,1)}, u32[]{:S(2)}) copy-start(bf16[1,2,768,2048]{3,2,1,0:T(8,128)(2,1)} %all-gather.5.cloned.1.call-done) | copy-start | bytes 18874372
  147.9 6.4 %copy-start.8 = (f32[384,768]{1,0:T(8,128)S(1)}, f32[384,768]{1,0:T(8,128)}, u32[]{:S(2)}) copy-start(f32[384,768]{1,0:T(8,128)} %fusion.5) | copy-start | bytes 3538948
  147.9 6.4 %copy-start.9 = (f32[384,768]{1,0:T(8,128)S(1)}, f32[384,768]{1,0:T(8,128)}, u32[]{:S(2)}) copy-start(f32[384,768]{1,0:T(8,128)} %fusion.3) | copy-start | bytes 3538948
  148.6 14.8 %all-to-all-start.4 = ((bf16[16,1,24]{2,1,0:T(2,128)(2,1)}), bf16[16,1,24]{2,1,0:T(2,128)(2,1)S(1)}, u32[]{:S(2)}, u32[]{:S(2)}) async-start(bf16[16,1,24]{2,1,0:T(2,128)(2,1)} %convert_element_type.97), calls=%async_computation.4 | async-start | bytes 16384 | tf_op jit(solution)/shard_map/all_to_all | solution.py:92
  154.3 4.4 %copy-start.10 = (f32[384,768]{1,0:T(8,128)S(1)}, f32[384,768]{1,0:T(8,128)}, u32[]{:S(2)}) copy-start(f32[384,768]{1,0:T(8,128)} %get-tuple-element.36) | copy-start | bytes 3538948
  163.4 38.0 %all-to-all-start.3 = ((bf16[16,24,2048]{2,1,0:T(8,128)(2,1)}), bf16[16,24,2048]{2,1,0:T(8,128)(2,1)S(1)}, u32[]{:S(2)}, u32[]{:S(2)}) async-start(bf16[16,24,2048]{2,1,0:T(8,128)(2,1)} %bitcast.12), calls=%async_computation.3 | async-start | bytes 3145728 | tf_op jit(solution)/shard_map/all_to_all | solution.py:85
  202.8 73.6 %copy-start.2 = (bf16[1,32,2048]{2,1,0:T(8,128)(2,1)S(1)}, bf16[1,32,2048]{2,1,0:T(8,128)(2,1)}, u32[]{:S(2)}) copy-start(bf16[1,32,2048]{2,1,0:T(8,128)(2,1)} %param.10) | copy-start | bytes 393220
Sparse Core Ops, SparseCore 0:
  9.6 83.0 all-gather.4
  94.2 44.9 all-gather.2
  148.0 43.3 reduce-scatter.1
